TPU v7x, 32 devices: a whole 2x2x4 slice. The times are simulated.
32 devices in a mesh: dp: 4 (over y, x), tensor: 8 (over z, core).
Axes of the slice: x: 2, y: 2, z: 4, core: 2. Of those that a mesh axis runs over, the one named last changes fastest.
Arguments:
- hidden_in: bfloat16 [12, 1024, 2048], P('dp', 'tensor'), may hold values from -6 to 6
- out_grad: bfloat16 [12, 1024, 2048], P('dp', 'tensor'), may hold values from -6 to 6
- buckets: int32 [1024, 1024], replicated, may hold values from 0 to 31
- gain_attn: bfloat16 [2048], replicated, may hold values from 0.099609375 to 1.8984375
- gain_ffn: bfloat16 [2048], replicated, may hold values from 0.099609375 to 1.8984375
- w_query: bfloat16 [2048, 2048], P('dp', 'tensor'), may hold values from -0.03125 to 0.03125
- w_key: bfloat16 [2048, 2048], P('dp', 'tensor'), may hold values from -0.125 to 0.125
- w_value: bfloat16 [2048, 2048], P('dp', 'tensor'), may hold values from -0.125 to 0.125
- w_out: bfloat16 [2048, 2048], P('tensor', 'dp'), may hold values from -1 to 1
- w_gate: bfloat16 [2048, 5120], P('dp', 'tensor'), may hold values from -0.125 to 0.125
- w_up: bfloat16 [2048, 5120], P('dp', 'tensor'), may hold values from -0.125 to 0.125
- w_down: bfloat16 [5120, 2048], P('tensor', 'dp'), may hold values from -0.125 to 0.125
- bias_table: bfloat16 [32, 32], P('dp', 'tensor'), may hold values from -4 to 4
Outputs:
- output: bfloat16 [12, 1024, 2048], P('dp', 'tensor')
- grad_input: bfloat16 [12, 1024, 2048], P('dp', 'tensor')
- grad_gain_attn: float32 [2048], replicated
- grad_gain_ffn: float32 [2048], replicated
- grad_query: float32 [2048, 2048], P('dp', 'tensor')
- grad_key: float32 [2048, 2048], P('dp', 'tensor')
- grad_value: float32 [2048, 2048], P('dp', 'tensor')
- grad_out: float32 [2048, 2048], P('tensor', 'dp')
- grad_gate: float32 [2048, 5120], P('dp', 'tensor')
- grad_up: float32 [2048, 5120], P('dp', 'tensor')
- grad_down: float32 [5120, 2048], P('tensor', 'dp')
- grad_bias: float32 [32, 32], P('dp', 'tensor')
Inputs may be any that keep to these rules, and one draw needn't show every extreme that they name: `buckets`: the bucket of each pair of query and key positions, the same for every sequence and head.
All inputs are finite; a program needn't handle non-finite values.
Results may differ from a plain program's by a relative error of at most 0.018.
Values may be sent and summed in bfloat16 or wider, within the bound.
No kernel may reach another device: no remote copies, remote signals or barrier semaphores. Data moves between devices by JAX's collectives and lax.ppermute only.
A program may use at most 320 MiB of HBM per device.

v0:
```python
import jax
import jax.numpy as jnp
from jax import lax
from jax.sharding import PartitionSpec as P

HD = 64
norm_eps = 1e-06
FULL_PRECISION = lax.Precision.HIGHEST


def rms_parts(seq_rows, gain_vec):
    inv_rms = lax.rsqrt(jnp.mean(seq_rows * seq_rows, axis=-1, keepdims=True) + norm_eps)
    plain_rows = seq_rows * inv_rms
    return (plain_rows, inv_rms, (plain_rows * gain_vec).astype(jnp.bfloat16))


def rms_back(grad_norm, plain_rows, inv_rms, gain_vec):
    scaled_grad = grad_norm * gain_vec
    return inv_rms * (
        scaled_grad - plain_rows * jnp.mean(scaled_grad * plain_rows, axis=-1, keepdims=True)
    )


def gelu_gate(gate_pre, up_pre):
    return jax.nn.gelu(gate_pre, approximate=True) * up_pre


def contract_rows(left_mat, right_mat):
    return lax.dot_general(
        left_mat, right_mat, (((0,), (0,)), ((), ())), preferred_element_type=jnp.float32
    )


def times_transpose(left_mat, right_mat):
    return lax.dot_general(
        left_mat, right_mat, (((1,), (1,)), ((), ())), preferred_element_type=jnp.float32
    )


def gather_norm(normed):
    return lax.all_gather(normed, "tensor", axis=0, tiled=True)


def gather_grad(grad_rows):
    return lax.all_gather(grad_rows, "tensor", axis=0, tiled=True)


def branch_sum(left_mat, right_mat):
    return lax.psum_scatter(
        jnp.dot(left_mat, right_mat, preferred_element_type=jnp.float32),
        "tensor",
        scatter_dimension=0,
        tiled=True,
    )


def input_sum(left_mat, right_mat):
    return lax.psum_scatter(
        times_transpose(left_mat, right_mat), "tensor", scatter_dimension=0, tiled=True
    )


def expand_bias(buckets, bias_cols):
    length = buckets.shape[0]
    block_rows = min(64, length)
    bucket_ids = jnp.arange(bias_cols.shape[0], dtype=jnp.int32)[None, :, None]

    def expand_one_block(bucket_rows):
        onehot = (bucket_rows[:, None, :] == bucket_ids).astype(jnp.float32)
        return jnp.einsum("ibj,bh->ihj", onehot, bias_cols, precision=FULL_PRECISION)

    blocks = lax.map(expand_one_block, buckets.reshape(length // block_rows, block_rows, length))
    return blocks.reshape(length, bias_cols.shape[1], length)


def bias_grad(buckets, grad_accum, bucket_count):
    length = buckets.shape[0]
    local_heads = grad_accum.shape[1]
    block_rows = min(64, length)
    bucket_ids = jnp.arange(bucket_count, dtype=jnp.int32)[None, :, None]

    def bias_one_block(carried, block_pair):
        bucket_rows, grad_rows = block_pair
        onehot = (bucket_rows[:, None, :] == bucket_ids).astype(jnp.float32)
        return (
            carried + jnp.einsum("ibj,ihj->bh", onehot, grad_rows, precision=FULL_PRECISION),
            None,
        )

    stacked = (
        buckets.reshape(length // block_rows, block_rows, length),
        grad_accum.reshape(length // block_rows, block_rows, local_heads, length),
    )
    total, _ = lax.scan(
        bias_one_block, jnp.zeros((bucket_count, local_heads), jnp.float32), stacked
    )
    return total


def body(
    hidden_in,
    out_grad,
    buckets,
    gain_attn,
    gain_ffn,
    w_query,
    w_key,
    w_value,
    w_out,
    w_gate,
    w_up,
    w_down,
    bias_table,
):
    query_cols, key_cols, value_cols, out_rows, gate_cols, up_cols, down_rows, bias_cols = (
        lax.all_gather(w_query, "dp", axis=0, tiled=True),
        lax.all_gather(w_key, "dp", axis=0, tiled=True),
        lax.all_gather(w_value, "dp", axis=0, tiled=True),
        lax.all_gather(w_out, "dp", axis=1, tiled=True),
        lax.all_gather(w_gate, "dp", axis=0, tiled=True),
        lax.all_gather(w_up, "dp", axis=0, tiled=True),
        lax.all_gather(w_down, "dp", axis=1, tiled=True),
        lax.all_gather(bias_table, "dp", axis=0, tiled=True),
    )
    gain_one = gain_attn.astype(jnp.float32)
    gain_two = gain_ffn.astype(jnp.float32)
    w_qkv = jnp.concatenate([query_cols, key_cols, value_cols], axis=1)
    w_ffn = jnp.concatenate([gate_cols, up_cols], axis=1)
    local_inner = query_cols.shape[1]
    local_heads = local_inner // HD
    local_ff = gate_cols.shape[1]
    seq_len = buckets.shape[0]
    model_dim = hidden_in.shape[2]
    block_len = min(512, seq_len)
    block_starts = list(range(0, seq_len, block_len))
    bias_full = expand_bias(buckets, bias_cols.astype(jnp.float32))
    out_initial = jnp.zeros((local_inner, model_dim), jnp.float32)

    def block_scores(queries, key_rows, row_start):
        query_block = queries[row_start : row_start + block_len]
        scores = jnp.einsum(
            "ihd,jhd->ihj", query_block, key_rows, preferred_element_type=jnp.float32
        )
        return (query_block, scores + bias_full[row_start : row_start + block_len])

    def micro_step(carried, scan_pair):
        grad_qkv, grad_outw, grad_ffn, grad_downw, grad_gone, grad_gtwo, grad_table = carried
        seq_in, seq_cot = scan_pair
        seq_rows = seq_in.astype(jnp.float32)
        plain_one, inv_one, norm_one = rms_parts(seq_rows, gain_one)
        norm_full = gather_norm(norm_one)
        projected = jnp.dot(norm_full, w_qkv, preferred_element_type=jnp.float32).astype(
            jnp.bfloat16
        )
        queries = projected[:, :local_inner].reshape(seq_len, local_heads, HD)
        key_rows = projected[:, local_inner : 2 * local_inner].reshape(seq_len, local_heads, HD)
        value_rows = projected[:, 2 * local_inner :].reshape(seq_len, local_heads, HD)
        context_parts = []
        lse_parts = []
        for row_start in block_starts:
            query_block, scores = block_scores(queries, key_rows, row_start)
            top_score = jnp.max(scores, axis=-1, keepdims=True)
            shifted = jnp.exp(scores - top_score)
            totals = jnp.sum(shifted, axis=-1, keepdims=True)
            attn_probs = shifted / totals
            lse_parts.append(top_score + jnp.log(totals))
            context_parts.append(
                jnp.einsum(
                    "ihj,jhd->ihd",
                    attn_probs.astype(jnp.bfloat16),
                    value_rows,
                    preferred_element_type=jnp.float32,
                ).astype(jnp.bfloat16)
            )
        context = jnp.concatenate(context_parts, axis=0).reshape(seq_len, local_inner)
        attn_rows = branch_sum(context, out_rows)
        mid_rows = seq_rows + attn_rows
        plain_two, inv_two, norm_two = rms_parts(mid_rows, gain_two)
        norm_full_two = gather_norm(norm_two)
        pre_ffn = jnp.dot(norm_full_two, w_ffn, preferred_element_type=jnp.float32)
        gate_pre = pre_ffn[:, :local_ff]
        up_pre = pre_ffn[:, local_ff:]
        hidden = gelu_gate(gate_pre, up_pre).astype(jnp.bfloat16)
        ffn_rows = branch_sum(hidden, down_rows)
        seq_out = (mid_rows + ffn_rows).astype(jnp.bfloat16)
        cot_full = gather_grad(seq_cot)
        grad_downw = grad_downw + contract_rows(hidden, cot_full)
        grad_hidden = times_transpose(cot_full, down_rows)
        _, gelu_pull = jax.vjp(gelu_gate, gate_pre, up_pre)
        grad_gate_pre, grad_up_pre = gelu_pull(grad_hidden)
        grad_pre = jnp.concatenate([grad_gate_pre, grad_up_pre], axis=1).astype(jnp.bfloat16)
        grad_ffn = grad_ffn + contract_rows(norm_full_two, grad_pre)
        grad_norm_two = input_sum(grad_pre, w_ffn)
        grad_gtwo = grad_gtwo + jnp.sum(grad_norm_two * plain_two, axis=0)
        grad_mid = seq_cot.astype(jnp.float32) + rms_back(
            grad_norm_two, plain_two, inv_two, gain_two
        )
        grad_mid_low = grad_mid.astype(jnp.bfloat16)
        grad_full = gather_grad(grad_mid_low)
        grad_context = times_transpose(grad_full, out_rows).astype(jnp.bfloat16)
        grad_outw = grad_outw + contract_rows(context, grad_full)
        grad_context = grad_context.reshape(seq_len, local_heads, HD)
        grad_query_parts = []
        grad_keys = jnp.zeros((seq_len, local_heads, HD), jnp.float32)
        grad_values = jnp.zeros((seq_len, local_heads, HD), jnp.float32)
        for block_index, row_start in enumerate(block_starts):
            query_block, scores = block_scores(queries, key_rows, row_start)
            attn_probs = jnp.exp(scores - lse_parts[block_index])
            probs_low = attn_probs.astype(jnp.bfloat16)
            grad_block = grad_context[row_start : row_start + block_len]
            grad_probs = jnp.einsum(
                "ihd,jhd->ihj", grad_block, value_rows, preferred_element_type=jnp.float32
            )
            row_inner = jnp.sum(attn_probs * grad_probs, axis=-1, keepdims=True)
            grad_scores = (attn_probs * (grad_probs - row_inner)).astype(jnp.bfloat16)
            grad_table = grad_table.at[row_start : row_start + block_len].add(
                grad_scores.astype(jnp.float32)
            )
            grad_query_parts.append(
                jnp.einsum(
                    "ihj,jhd->ihd", grad_scores, key_rows, preferred_element_type=jnp.float32
                )
            )
            grad_keys = grad_keys + jnp.einsum(
                "ihj,ihd->jhd", grad_scores, query_block, preferred_element_type=jnp.float32
            )
            grad_values = grad_values + jnp.einsum(
                "ihj,ihd->jhd", probs_low, grad_block, preferred_element_type=jnp.float32
            )
        grad_queries = jnp.concatenate(grad_query_parts, axis=0)
        grad_proj = jnp.concatenate(
            [
                grad_queries.reshape(seq_len, local_inner),
                grad_keys.reshape(seq_len, local_inner),
                grad_values.reshape(seq_len, local_inner),
            ],
            axis=1,
        ).astype(jnp.bfloat16)
        grad_qkv = grad_qkv + contract_rows(norm_full, grad_proj)
        grad_norm_one = input_sum(grad_proj, w_qkv)
        grad_gone = grad_gone + jnp.sum(grad_norm_one * plain_one, axis=0)
        grad_in = (grad_mid + rms_back(grad_norm_one, plain_one, inv_one, gain_one)).astype(
            jnp.bfloat16
        )
        new_carry = (grad_qkv, grad_outw, grad_ffn, grad_downw, grad_gone, grad_gtwo, grad_table)
        return (new_carry, (seq_out, grad_in))

    initial = (
        jnp.zeros((model_dim, 3 * local_inner), jnp.float32),
        out_initial,
        jnp.zeros((model_dim, 2 * local_ff), jnp.float32),
        jnp.zeros((local_ff, model_dim), jnp.float32),
        jnp.zeros((model_dim,), jnp.float32),
        jnp.zeros((model_dim,), jnp.float32),
        jnp.zeros((seq_len, local_heads, seq_len), jnp.float32),
    )
    final_carry, (outputs_seq, grads_seq) = lax.scan(micro_step, initial, (hidden_in, out_grad))
    grad_qkv, grad_outw, grad_ffn, grad_downw, grad_gone, grad_gtwo, grad_table = final_carry
    table_grad = bias_grad(buckets, grad_table, bias_cols.shape[0])
    shards = (
        lax.psum_scatter(
            grad_qkv[:, :local_inner].astype(jnp.bfloat16), "dp", scatter_dimension=0, tiled=True
        ).astype(jnp.float32),
        lax.psum_scatter(
            grad_qkv[:, local_inner : 2 * local_inner].astype(jnp.bfloat16),
            "dp",
            scatter_dimension=0,
            tiled=True,
        ).astype(jnp.float32),
        lax.psum_scatter(
            grad_qkv[:, 2 * local_inner :].astype(jnp.bfloat16),
            "dp",
            scatter_dimension=0,
            tiled=True,
        ).astype(jnp.float32),
        lax.psum_scatter(
            grad_outw.astype(jnp.bfloat16), "dp", scatter_dimension=1, tiled=True
        ).astype(jnp.float32),
        lax.psum_scatter(
            grad_ffn[:, :local_ff].astype(jnp.bfloat16), "dp", scatter_dimension=0, tiled=True
        ).astype(jnp.float32),
        lax.psum_scatter(
            grad_ffn[:, local_ff:].astype(jnp.bfloat16), "dp", scatter_dimension=0, tiled=True
        ).astype(jnp.float32),
        lax.psum_scatter(
            grad_downw.astype(jnp.bfloat16), "dp", scatter_dimension=1, tiled=True
        ).astype(jnp.float32),
        lax.psum_scatter(
            table_grad.astype(jnp.bfloat16), "dp", scatter_dimension=0, tiled=True
        ).astype(jnp.float32),
    )
    gain_sums = lax.psum((grad_gone, grad_gtwo), ("dp", "tensor"))
    return (
        outputs_seq,
        grads_seq,
        gain_sums[0],
        gain_sums[1],
        shards[0],
        shards[1],
        shards[2],
        shards[3],
        shards[4],
        shards[5],
        shards[6],
        shards[7],
    )


def solution(mesh):
    in_specs = (
        P("dp", "tensor", None),
        P("dp", "tensor", None),
        P(),
        P(),
        P(),
        P("dp", "tensor"),
        P("dp", "tensor"),
        P("dp", "tensor"),
        P("tensor", "dp"),
        P("dp", "tensor"),
        P("dp", "tensor"),
        P("tensor", "dp"),
        P("dp", "tensor"),
    )
    out_specs = (
        P("dp", "tensor", None),
        P("dp", "tensor", None),
        P(),
        P(),
        P("dp", "tensor"),
        P("dp", "tensor"),
        P("dp", "tensor"),
        P("tensor", "dp"),
        P("dp", "tensor"),
        P("dp", "tensor"),
        P("tensor", "dp"),
        P("dp", "tensor"),
    )
    return jax.shard_map(body, mesh=mesh, in_specs=in_specs, out_specs=out_specs, check_vma=False)
```

profile of v0, /device:TPU:0, one launch (start us, length us, event | category | flops | bytes accessed | tf_op | source)
XLA Modules:
  0.0 2525.8 jit_solution(10109821729811257224)
XLA Ops:
  21.7 73.3 %while.53 = (s32[]{:T(128)}, f32[16,64,4,1024]{3,2,1,0:T(4,128)}, s32[16,64,1024]{2,1,0:T(8,128)}, f32[32,4]{0,1:T(4,128)S(1)}, s32[]{:T(128)}) while((s32[]{:T(128)}, f32[16,64,4,1024]{3,2,1,0:T(4,128)}, s32[16,64,1024]{2,1,0:T(8,128)}, f32[32,4]{0,1:T(4,128)S(1)}, s32[]{:T(128)}) %tuple.177), condition=%wide.region_1.2_spmd.clone, body=%wide.region_0.1_spmd.clone.sunk | while | flops 102760448 | bytes 1835597 | solution.py:72
  137.1 41.2 %all-gather.29.cloned.1.call-done = bf16[2048,640]{1,0:T(8,128)(2,1)} async-done(((bf16[512,640]{1,0:T(8,128)(2,1)}), bf16[2048,640]{1,0:T(8,128)(2,1)}) %all-gather.29.cloned.1.call-update) | async-done | bytes 2621456 | tf_op jit(solution)/shard_map/all_gather | solution.py:121
  183.6 22.7 all-gather.23.cloned.1.call-done
  206.4 41.2 %all-gather.25.cloned.1.call-done = bf16[640,2048]{1,0:T(8,128)(2,1)} async-done(((bf16[640,512]{1,0:T(8,128)(2,1)}), bf16[640,2048]{1,0:T(8,128)(2,1)}) %all-gather.25.cloned.1.call-update) | async-done | bytes 2621456 | tf_op jit(solution)/shard_map/all_gather | solution.py:122
  255.5 2008.2 %while.54 = (s32[]{:T(128)}, f32[2048,768]{1,0:T(8,128)}, f32[256,2048]{1,0:T(8,128)}, f32[2048,1280]{1,0:T(8,128)}, f32[640,2048]{1,0:T(8,128)}, /*index=5*/f32...) while((s32[]{:T(128)}, f32[2048,768]{1,0:T(8,128)}, ...), condition=%wide.region_19.20_spmd.clone, body=%wide.region_2.19_spmd.clone.sunk | while | flops 40408182784 | bytes 830275520 | solution.py:257
  258.9 47.0 %all-gather.31.cloned.1.call-done = bf16[1024,2048]{1,0:T(8,128)(2,1)} async-done(((bf16[128,2048]{1,0:T(8,128)(2,1)}), bf16[1024,2048]{1,0:T(8,128)(2,1)}) %all-gather.31.cloned.1.call-update) | async-done | bytes 4194320 | tf_op jit(solution)/shard_map/while/body/eval_jaxpr/all_gather | solution.py:41
  336.9 88.4 %reduce-scatter.27.cloned.1.call-done = f32[128,2048]{1,0:T(8,128)} async-done(((f32[1024,2048]{1,0:T(8,128)}), f32[128,2048]{1,0:T(8,128)}) %reduce-scatter.27.cloned.1.call-update) | async-done | bytes 1048592 | tf_op jit(solution)/shard_map/while/body/eval_jaxpr/reduce_scatter | solution.py:49
  429.9 43.5 %all-gather.33.cloned.1.call-done = bf16[1024,2048]{1,0:T(8,128)(2,1)} async-done(((bf16[128,2048]{1,0:T(8,128)(2,1)}), bf16[1024,2048]{1,0:T(8,128)(2,1)}) %all-gather.33.cloned.1.call-update) | async-done | bytes 4194320 | tf_op jit(solution)/shard_map/while/body/eval_jaxpr/all_gather | solution.py:41
  483.7 37.6 %all-gather.35.cloned.1.call-done = bf16[1,1024,2048]{2,1,0:T(8,128)(2,1)} async-done(((bf16[1,128,2048]{2,1,0:T(8,128)(2,1)}), bf16[1,1024,2048]{2,1,0:T(8,128)(2,1)}) %all-gather.35.cloned.1.call-update) | async-done | bytes 4194320 | tf_op jit(solution)/shard_map/while/body/eval_jaxpr/all_gather | solution.py:45
  543.5 88.5 %reduce-scatter.29.cloned.1.call-done = f32[128,2048]{1,0:T(8,128)} async-done(((f32[1024,2048]{1,0:T(8,128)}), f32[128,2048]{1,0:T(8,128)}) %reduce-scatter.29.cloned.1.call-update) | async-done | bytes 1048592 | tf_op jit(solution)/shard_map/while/body/eval_jaxpr/reduce_scatter | solution.py:58
  637.0 45.2 %all-gather.37.cloned.1.call-done = bf16[1024,2048]{1,0:T(8,128)(2,1)} async-done(((bf16[128,2048]{1,0:T(8,128)(2,1)}), bf16[1024,2048]{1,0:T(8,128)(2,1)}) %all-gather.37.cloned.1.call-update) | async-done | bytes 4194320 | tf_op jit(solution)/shard_map/while/body/eval_jaxpr/all_gather | solution.py:45
  776.3 53.9 %reduce-scatter.31.cloned.1.call-done = f32[128,2048]{1,0:T(8,128)} async-done(((f32[1024,2048]{1,0:T(8,128)}), f32[128,2048]{1,0:T(8,128)}) %reduce-scatter.31.cloned.1.call-update) | async-done | bytes 1048592 | tf_op jit(solution)/shard_map/while/body/eval_jaxpr/reduce_scatter | solution.py:58
  831.9 88.4 %reduce-scatter.33.cloned.1.call-done = f32[128,2048]{1,0:T(8,128)} async-done(((f32[1024,2048]{1,0:T(8,128)}), f32[128,2048]{1,0:T(8,128)}) %reduce-scatter.33.cloned.1.call-update) | async-done | bytes 1048592 | tf_op jit(solution)/shard_map/while/body/eval_jaxpr/reduce_scatter | solution.py:49
  927.3 45.4 %all-gather.31.cloned.1.call-done = bf16[1024,2048]{1,0:T(8,128)(2,1)} async-done(((bf16[128,2048]{1,0:T(8,128)(2,1)}), bf16[1024,2048]{1,0:T(8,128)(2,1)}) %all-gather.31.cloned.1.call-update) | async-done | bytes 4194320 | tf_op jit(solution)/shard_map/while/body/eval_jaxpr/all_gather | solution.py:41
  1003.7 88.4 %reduce-scatter.27.cloned.1.call-done = f32[128,2048]{1,0:T(8,128)} async-done(((f32[1024,2048]{1,0:T(8,128)}), f32[128,2048]{1,0:T(8,128)}) %reduce-scatter.27.cloned.1.call-update) | async-done | bytes 1048592 | tf_op jit(solution)/shard_map/while/body/eval_jaxpr/reduce_scatter | solution.py:49
  1096.8 43.5 %all-gather.33.cloned.1.call-done = bf16[1024,2048]{1,0:T(8,128)(2,1)} async-done(((bf16[128,2048]{1,0:T(8,128)(2,1)}), bf16[1024,2048]{1,0:T(8,128)(2,1)}) %all-gather.33.cloned.1.call-update) | async-done | bytes 4194320 | tf_op jit(solution)/shard_map/while/body/eval_jaxpr/all_gather | solution.py:41
  1150.6 37.6 %all-gather.35.cloned.1.call-done = bf16[1,1024,2048]{2,1,0:T(8,128)(2,1)} async-done(((bf16[1,128,2048]{2,1,0:T(8,128)(2,1)}), bf16[1,1024,2048]{2,1,0:T(8,128)(2,1)}) %all-gather.35.cloned.1.call-update) | async-done | bytes 4194320 | tf_op jit(solution)/shard_map/while/body/eval_jaxpr/all_gather | solution.py:45
  1210.4 88.4 %reduce-scatter.29.cloned.1.call-done = f32[128,2048]{1,0:T(8,128)} async-done(((f32[1024,2048]{1,0:T(8,128)}), f32[128,2048]{1,0:T(8,128)}) %reduce-scatter.29.cloned.1.call-update) | async-done | bytes 1048592 | tf_op jit(solution)/shard_map/while/body/eval_jaxpr/reduce_scatter | solution.py:58
  1303.8 45.2 %all-gather.37.cloned.1.call-done = bf16[1024,2048]{1,0:T(8,128)(2,1)} async-done(((bf16[128,2048]{1,0:T(8,128)(2,1)}), bf16[1024,2048]{1,0:T(8,128)(2,1)}) %all-gather.37.cloned.1.call-update) | async-done | bytes 4194320 | tf_op jit(solution)/shard_map/while/body/eval_jaxpr/all_gather | solution.py:45
  1449.5 47.5 %reduce-scatter.31.cloned.1.call-done = f32[128,2048]{1,0:T(8,128)} async-done(((f32[1024,2048]{1,0:T(8,128)}), f32[128,2048]{1,0:T(8,128)}) %reduce-scatter.31.cloned.1.call-update) | async-done | bytes 1048592 | tf_op jit(solution)/shard_map/while/body/eval_jaxpr/reduce_scatter | solution.py:58
  1498.8 88.5 %reduce-scatter.33.cloned.1.call-done = f32[128,2048]{1,0:T(8,128)} async-done(((f32[1024,2048]{1,0:T(8,128)}), f32[128,2048]{1,0:T(8,128)}) %reduce-scatter.33.cloned.1.call-update) | async-done | bytes 1048592 | tf_op jit(solution)/shard_map/while/body/eval_jaxpr/reduce_scatter | solution.py:49
  1594.3 45.4 %all-gather.31.cloned.1.call-done = bf16[1024,2048]{1,0:T(8,128)(2,1)} async-done(((bf16[128,2048]{1,0:T(8,128)(2,1)}), bf16[1024,2048]{1,0:T(8,128)(2,1)}) %all-gather.31.cloned.1.call-update) | async-done | bytes 4194320 | tf_op jit(solution)/shard_map/while/body/eval_jaxpr/all_gather | solution.py:41
  1670.8 88.4 %reduce-scatter.27.cloned.1.call-done = f32[128,2048]{1,0:T(8,128)} async-done(((f32[1024,2048]{1,0:T(8,128)}), f32[128,2048]{1,0:T(8,128)}) %reduce-scatter.27.cloned.1.call-update) | async-done | bytes 1048592 | tf_op jit(solution)/shard_map/while/body/eval_jaxpr/reduce_scatter | solution.py:49
  1763.8 43.5 %all-gather.33.cloned.1.call-done = bf16[1024,2048]{1,0:T(8,128)(2,1)} async-done(((bf16[128,2048]{1,0:T(8,128)(2,1)}), bf16[1024,2048]{1,0:T(8,128)(2,1)}) %all-gather.33.cloned.1.call-update) | async-done | bytes 4194320 | tf_op jit(solution)/shard_map/while/body/eval_jaxpr/all_gather | solution.py:41
  1817.6 37.4 %all-gather.35.cloned.1.call-done = bf16[1,1024,2048]{2,1,0:T(8,128)(2,1)} async-done(((bf16[1,128,2048]{2,1,0:T(8,128)(2,1)}), bf16[1,1024,2048]{2,1,0:T(8,128)(2,1)}) %all-gather.35.cloned.1.call-update) | async-done | bytes 4194320 | tf_op jit(solution)/shard_map/while/body/eval_jaxpr/all_gather | solution.py:45
  1877.3 88.4 %reduce-scatter.29.cloned.1.call-done = f32[128,2048]{1,0:T(8,128)} async-done(((f32[1024,2048]{1,0:T(8,128)}), f32[128,2048]{1,0:T(8,128)}) %reduce-scatter.29.cloned.1.call-update) | async-done | bytes 1048592 | tf_op jit(solution)/shard_map/while/body/eval_jaxpr/reduce_scatter | solution.py:58
  1970.7 45.2 %all-gather.37.cloned.1.call-done = bf16[1024,2048]{1,0:T(8,128)(2,1)} async-done(((bf16[128,2048]{1,0:T(8,128)(2,1)}), bf16[1024,2048]{1,0:T(8,128)(2,1)}) %all-gather.37.cloned.1.call-update) | async-done | bytes 4194320 | tf_op jit(solution)/shard_map/while/body/eval_jaxpr/all_gather | solution.py:45
  2116.3 47.5 %reduce-scatter.31.cloned.1.call-done = f32[128,2048]{1,0:T(8,128)} async-done(((f32[1024,2048]{1,0:T(8,128)}), f32[128,2048]{1,0:T(8,128)}) %reduce-scatter.31.cloned.1.call-update) | async-done | bytes 1048592 | tf_op jit(solution)/shard_map/while/body/eval_jaxpr/reduce_scatter | solution.py:58
  2165.6 88.6 %reduce-scatter.33.cloned.1.call-done = f32[128,2048]{1,0:T(8,128)} async-done(((f32[1024,2048]{1,0:T(8,128)}), f32[128,2048]{1,0:T(8,128)}) %reduce-scatter.33.cloned.1.call-update) | async-done | bytes 1048592 | tf_op jit(solution)/shard_map/while/body/eval_jaxpr/reduce_scatter | solution.py:49
  2306.5 104.5 %while.55 = (s32[]{:T(128)}, f32[32,4]{0,1:T(4,128)S(1)}, s32[16,64,1024]{2,1,0:T(8,128)}, f32[16,64,4,1024]{3,2,1,0:T(4,128)}, s32[]{:T(128)}, /*index=5*/s32[]{:T(128)}) while((s32[]{:T(128)}, f32[32,4]{0,1:T(4,128)S(1)}, s32[16,64,1024]{2,1,0:T(8,128)}, f32[16,64,4,1024]{3,2,1,0:T(4,128)}, s32[]{:T(128)}, ...), condition=%wide.region_30.31_spmd.clone, body=%wide.region_29.30_spmd.clone.sunk | while | flops 102760704 | bytes 1836127 | solution.py:94
  2420.8 37.9 %all-reduce.1 = (f32[2048]{0:T(1024)}, f32[2048]{0:T(1024)}) all-reduce(f32[2048]{0:T(1024)S(1)} %copy-done.26, f32[2048]{0:T(1024)S(1)} %copy-done.23), channel_id=1, replica_groups=mesh['dp'=4,'tensor'=8] {'dp','tensor'}, use_global_device_ids=true, to_apply=%region_20.21 | all-reduce | flops 4096 | bytes 32768 | tf_op jit(solution)/shard_map/psum | solution.py:292
  2476.4 40.4 %reduce-scatter.23.cloned.1.call-done = bf16[512,640]{1,0:T(8,128)(2,1)} async-done(((bf16[2048,640]{1,0:T(8,128)(2,1)}), bf16[512,640]{1,0:T(8,128)(2,1)}) %reduce-scatter.23.cloned.1.call-update) | async-done | bytes 655376 | tf_op jit(solution)/shard_map/reduce_scatter | solution.py:282
  (599 shorter events, 857.4 us)
Async XLA Ops:
  7.2 107.2 %all-gather.17.cloned.1.call-start = ((), (), s32[]{:S(2)}) async-start(), calls=%async_computation.11 | async-start | bytes 1310720 | tf_op jit(solution)/shard_map/all_gather | solution.py:116
  7.9 106.5 %all-gather.19.cloned.1.call-start = ((), (), s32[]{:S(2)}) async-start(), calls=%async_computation.12 | async-start | bytes 1310720 | tf_op jit(solution)/shard_map/all_gather | solution.py:117
  8.7 105.7 %all-gather.21.cloned.1.call-start = ((), (), s32[]{:S(2)}) async-start(), calls=%async_computation.13 | async-start | bytes 1310720 | tf_op jit(solution)/shard_map/all_gather | solution.py:118
  9.4 127.7 %all-gather.27.cloned.1.call-start = ((), (), s32[]{:S(2)}) async-start(), calls=%async_computation.16 | async-start | bytes 3276800 | tf_op jit(solution)/shard_map/all_gather | solution.py:120
  10.0 168.3 %all-gather.29.cloned.1.call-start = ((), (), s32[]{:S(2)}) async-start(), calls=%async_computation.17 | async-start | bytes 3276800 | tf_op jit(solution)/shard_map/all_gather | solution.py:121
  10.6 195.8 %all-gather.23.cloned.1.call-start = ((), (), s32[]{:S(2)}) async-start(), calls=%async_computation.14 | async-start | bytes 1310720 | tf_op jit(solution)/shard_map/all_gather | solution.py:119
  11.1 236.5 %all-gather.25.cloned.1.call-start = ((), (), s32[]{:S(2)}) async-start(), calls=%async_computation.15 | async-start | bytes 3276800 | tf_op jit(solution)/shard_map/all_gather | solution.py:122
  258.8 166.5 %reduce-scatter.27.cloned.1.call-start = ((), (), s32[]{:S(2)}) async-start(), calls=%async_computation.26 | async-start | bytes 9437184 | tf_op jit(solution)/shard_map/while/body/eval_jaxpr/reduce_scatter | solution.py:49
  336.8 136.5 %all-gather.33.cloned.1.call-start = ((), (), s32[]{:S(2)}) async-start(), calls=%async_computation.27 | async-start | bytes 4718592 | tf_op jit(solution)/shard_map/while/body/eval_jaxpr/all_gather | solution.py:41
  429.8 202.2 %reduce-scatter.29.cloned.1.call-start = ((), (), s32[]{:S(2)}) async-start(), calls=%async_computation.29 | async-start | bytes 9437184 | tf_op jit(solution)/shard_map/while/body/eval_jaxpr/reduce_scatter | solution.py:58
  543.5 138.7 %all-gather.37.cloned.1.call-start = ((), (), s32[]{:S(2)}) async-start(), calls=%async_computation.30 | async-start | bytes 4718592 | tf_op jit(solution)/shard_map/while/body/eval_jaxpr/all_gather | solution.py:45
  636.7 193.4 %reduce-scatter.31.cloned.1.call-start = ((), (), s32[]{:S(2)}) async-start(), calls=%async_computation.31 | async-start | bytes 9437184 | tf_op jit(solution)/shard_map/while/body/eval_jaxpr/reduce_scatter | solution.py:58
  741.6 178.7 %reduce-scatter.33.cloned.1.call-start = ((), (), s32[]{:S(2)}) async-start(), calls=%async_computation.32 | async-start | bytes 9437184 | tf_op jit(solution)/shard_map/while/body/eval_jaxpr/reduce_scatter | solution.py:49
  927.2 164.9 %reduce-scatter.27.cloned.1.call-start = ((), (), s32[]{:S(2)}) async-start(), calls=%async_computation.26 | async-start | bytes 9437184 | tf_op jit(solution)/shard_map/while/body/eval_jaxpr/reduce_scatter | solution.py:49
  1003.7 136.6 %all-gather.33.cloned.1.call-start = ((), (), s32[]{:S(2)}) async-start(), calls=%async_computation.27 | async-start | bytes 4718592 | tf_op jit(solution)/shard_map/while/body/eval_jaxpr/all_gather | solution.py:41
  1096.7 202.2 %reduce-scatter.29.cloned.1.call-start = ((), (), s32[]{:S(2)}) async-start(), calls=%async_computation.29 | async-start | bytes 9437184 | tf_op jit(solution)/shard_map/while/body/eval_jaxpr/reduce_scatter | solution.py:58
  1210.4 138.7 %all-gather.37.cloned.1.call-start = ((), (), s32[]{:S(2)}) async-start(), calls=%async_computation.30 | async-start | bytes 4718592 | tf_op jit(solution)/shard_map/while/body/eval_jaxpr/all_gather | solution.py:45
  1303.6 193.4 %reduce-scatter.31.cloned.1.call-start = ((), (), s32[]{:S(2)}) async-start(), calls=%async_computation.31 | async-start | bytes 9437184 | tf_op jit(solution)/shard_map/while/body/eval_jaxpr/reduce_scatter | solution.py:58
  1408.5 178.8 %reduce-scatter.33.cloned.1.call-start = ((), (), s32[]{:S(2)}) async-start(), calls=%async_computation.32 | async-start | bytes 9437184 | tf_op jit(solution)/shard_map/while/body/eval_jaxpr/reduce_scatter | solution.py:49
  1594.2 164.9 %reduce-scatter.27.cloned.1.call-start = ((), (), s32[]{:S(2)}) async-start(), calls=%async_computation.26 | async-start | bytes 9437184 | tf_op jit(solution)/shard_map/while/body/eval_jaxpr/reduce_scatter | solution.py:49
  1670.7 136.5 %all-gather.33.cloned.1.call-start = ((), (), s32[]{:S(2)}) async-start(), calls=%async_computation.27 | async-start | bytes 4718592 | tf_op jit(solution)/shard_map/while/body/eval_jaxpr/all_gather | solution.py:41
  1763.7 202.0 %reduce-scatter.29.cloned.1.call-start = ((), (), s32[]{:S(2)}) async-start(), calls=%async_computation.29 | async-start | bytes 9437184 | tf_op jit(solution)/shard_map/while/body/eval_jaxpr/reduce_scatter | solution.py:58
  1877.2 138.7 %all-gather.37.cloned.1.call-start = ((), (), s32[]{:S(2)}) async-start(), calls=%async_computation.30 | async-start | bytes 4718592 | tf_op jit(solution)/shard_map/while/body/eval_jaxpr/all_gather | solution.py:45
  1970.4 193.4 %reduce-scatter.31.cloned.1.call-start = ((), (), s32[]{:S(2)}) async-start(), calls=%async_computation.31 | async-start | bytes 9437184 | tf_op jit(solution)/shard_map/while/body/eval_jaxpr/reduce_scatter | solution.py:58
  2075.3 178.8 %reduce-scatter.33.cloned.1.call-start = ((), (), s32[]{:S(2)}) async-start(), calls=%async_computation.32 | async-start | bytes 9437184 | tf_op jit(solution)/shard_map/while/body/eval_jaxpr/reduce_scatter | solution.py:49
  2263.7 195.7 %reduce-scatter.19.cloned.1.call-start = ((), (), s32[]{:S(2)}) async-start(), calls=%async_computation.21 | async-start | bytes 1310720 | tf_op jit(solution)/shard_map/reduce_scatter | solution.py:276
  2266.5 194.7 %reduce-scatter.13.cloned.1.call-start = ((), (), s32[]{:S(2)}) async-start(), calls=%async_computation.18 | async-start | bytes 1310720 | tf_op jit(solution)/shard_map/reduce_scatter | solution.py:261
  2271.4 191.6 %reduce-scatter.15.cloned.1.call-start = ((), (), s32[]{:S(2)}) async-start(), calls=%async_computation.19 | async-start | bytes 1310720 | tf_op jit(solution)/shard_map/reduce_scatter | solution.py:264
  2272.1 192.6 %reduce-scatter.17.cloned.1.call-start = ((), (), s32[]{:S(2)}) async-start(), calls=%async_computation.20 | async-start | bytes 1310720 | tf_op jit(solution)/shard_map/reduce_scatter | solution.py:270
  2272.9 193.7 %reduce-scatter.25.cloned.1.call-start = ((), (), s32[]{:S(2)}) async-start(), calls=%async_computation.24 | async-start | bytes 3276800 | tf_op jit(solution)/shard_map/reduce_scatter | solution.py:285
  2277.4 196.8 %reduce-scatter.21.cloned.1.call-start = ((), (), s32[]{:S(2)}) async-start(), calls=%async_computation.22 | async-start | bytes 3276800 | tf_op jit(solution)/shard_map/reduce_scatter | solution.py:279
  2284.9 231.9 %reduce-scatter.23.cloned.1.call-start = ((), (), s32[]{:S(2)}) async-start(), calls=%async_computation.23 | async-start | bytes 3276800 | tf_op jit(solution)/shard_map/reduce_scatter | solution.py:282
  (134 other events, 4881.2 us)
Sparse Core Ops, SparseCore 0:
  9.8 29.2 all-gather.16
  97.5 39.4 all-gather.26
  138.8 39.4 all-gather.28
  208.2 39.3 all-gather.24
  258.9 46.8 all-gather.30
  337.0 88.3 reduce-scatter.26
  428.0 45.3 all-gather.32
  475.5 45.6 all-gather.34
  543.6 88.3 reduce-scatter.28
  636.9 45.3 all-gather.36
  741.7 88.3 reduce-scatter.30
  832.3 87.9 reduce-scatter.32
  927.3 45.3 all-gather.30
  1003.8 88.3 reduce-scatter.26
  1094.9 45.3 all-gather.32
  1142.4 45.6 all-gather.34
  1210.5 88.3 reduce-scatter.28
  1303.7 45.3 all-gather.36
  1408.6 88.3 reduce-scatter.30
  1499.3 87.9 reduce-scatter.32
  1594.4 45.3 all-gather.30
  1670.8 88.3 reduce-scatter.26
  1761.9 45.3 all-gather.32
  1809.3 45.6 all-gather.34
  1877.3 88.3 reduce-scatter.28
  1970.6 45.3 all-gather.36
  2075.5 88.3 reduce-scatter.30
  2166.1 88.0 reduce-scatter.32
  2328.6 27.9 reduce-scatter.14
  2390.9 40.1 reduce-scatter.24
  2433.9 40.2 reduce-scatter.20
  2477.2 39.5 reduce-scatter.22
  (6 shorter events, 161.3 us)
where the time goes:
time: 2530 us
  waiting for transfers between devices  1640 us (65%)
  matrix products  548 us (22%)
  other arithmetic  151 us (6%)
  local copies, waits for them, and re-layouts  105 us (4%)
  blocking collectives  57.4 us (2%)
    reduce_scatter x6, waiting for transfers between devices, branch_sum(): lax.psum_scatter(jnp.dot(left_mat, right_mat, preferred_element_type=jnp....  531 us
    reduce_scatter x6, waiting for transfers between devices, input_sum(): lax.psum_scatter(times_transpose(left_mat, right_mat), 'tensor', scatter_...  414 us
    all_gather x6, waiting for transfers between devices, gather_norm(): return lax.all_gather(normed, 'tensor', axis=0, tiled=True)  268 us
    all_gather x6, waiting for transfers between devices, gather_grad(): return lax.all_gather(grad_rows, 'tensor', axis=0, tiled=True)  248 us
    dot_general x12, matrix products, times_transpose(): lax.dot_general(left_mat, right_mat, (((1,), (1,)), ((), ())), preferred_...  96.6 us
    dot_general x16, matrix products, bias_one_block(): jnp.einsum('ibj,ihj->bh', onehot, grad_rows, precision=FULL_PRECISION)  88.6 us
    dot_general x12, matrix products, contract_rows(): lax.dot_general(left_mat, right_mat, (((0,), (0,)), ((), ())), preferred_...  84.3 us
    scatter-add x6, other arithmetic, micro_step(): grad_table.at[row_start:row_start + block_len]  58.8 us
  transfers between devices with their start and end apart: 38, of which 30 were waited for; matrix products, arithmetic and copies ran while one was open for 16% of the time, Pallas kernels for 0%

commit v1 on v0

--- a/solution.py
+++ b/solution.py
@@ -2,10 +2,26 @@
 import jax.numpy as jnp
 from jax import lax
 from jax.sharding import PartitionSpec as P
+from jax.lax import axis_index, axis_size, ppermute
 
 HD = 64
 norm_eps = 1e-06
 FULL_PRECISION = lax.Precision.HIGHEST
+
+
+def frames_deliver(in_array, shard_axis):
+    carry_in = axis_size(shard_axis)
+    block_next, outcome_arr = (carry_in, axis_index(shard_axis))
+    carry, piece_next = (in_array, 1)
+    while piece_next < block_next:
+        arr_now = ppermute(
+            carry, shard_axis, [(dev_i, dev_i ^ piece_next) for dev_i in range(block_next)]
+        )
+        oldest = jnp.concatenate([carry, arr_now], axis=0)
+        placed = jnp.concatenate([arr_now, carry], axis=0)
+        carry = jnp.where(outcome_arr & piece_next == 0, oldest, placed)
+        piece_next = 2 * piece_next
+    return carry
 
 
 def rms_parts(seq_rows, gain_vec):
@@ -42,7 +58,7 @@
 
 
 def gather_grad(grad_rows):
-    return lax.all_gather(grad_rows, "tensor", axis=0, tiled=True)
+    return frames_deliver(grad_rows, "tensor")
 
 
 def branch_sum(left_mat, right_mat):

time: 2530 us -> 2950 us (1.17)
  waiting for transfers between devices: 1640 us -> 2040 us
    ppermute x0 -> x18, waiting for transfers between devices: none -> 791 us  [frames_deliver(): ppermute(carry, shard_axis, [(dev_i, dev_i ^ piece_next) for dev_i in ran...]
    all_gather x6 -> x0, waiting for transfers between devices: 248 us -> none  [gather_grad(): return lax.all_gather(grad_rows, 'tensor', axis=0, tiled=True)]
    all_gather x6, waiting for transfers between devices: 268 us -> 138 us  [gather_norm(): return lax.all_gather(normed, 'tensor', axis=0, tiled=True)]
  transfers between devices with their start and end apart: 38 -> 50, of which waited for: 30 -> 39; matrix products, arithmetic and copies ran while one was open for 16% -> 15% of each run, Pallas kernels for 0% -> 0%
where the time goes in v1:
time: 2950 us; the launch traced here: 2940 us
  waiting for transfers between devices  2040 us (69%)
  matrix products  529 us (18%)
  other arithmetic  174 us (6%)
  local copies, waits for them, and re-layouts  104 us (4%)
  blocking collectives  57.7 us (2%)
    ppermute x18, waiting for transfers between devices, frames_deliver(): ppermute(carry, shard_axis, [(dev_i, dev_i ^ piece_next) for dev_i in ran...  791 us
    reduce_scatter x6, waiting for transfers between devices, branch_sum(): lax.psum_scatter(jnp.dot(left_mat, right_mat, preferred_element_type=jnp....  531 us
    reduce_scatter x6, waiting for transfers between devices, input_sum(): lax.psum_scatter(times_transpose(left_mat, right_mat), 'tensor', scatter_...  409 us
    all_gather x6, waiting for transfers between devices, gather_norm(): return lax.all_gather(normed, 'tensor', axis=0, tiled=True)  138 us
    dot_general x12, matrix products, contract_rows(): lax.dot_general(left_mat, right_mat, (((0,), (0,)), ((), ())), preferred_...  88.8 us
    dot_general x16, matrix products, bias_one_block(): jnp.einsum('ibj,ihj->bh', onehot, grad_rows, precision=FULL_PRECISION)  88.6 us
    dot_general x12, matrix products, times_transpose(): lax.dot_general(left_mat, right_mat, (((1,), (1,)), ((), ())), preferred_...  84.6 us
  transfers between devices with their start and end apart: 50, of which 39 were waited for; matrix products, arithmetic and copies ran while one was open for 15% of the time, Pallas kernels for 0%

profile of v1, /device:TPU:0, one launch (start us, length us, event | category | flops | bytes accessed | tf_op | source)
XLA Modules:
  0.0 2938.1 jit_solution(1780639868508370534)
XLA Ops:
  21.7 73.3 %while.53 = (s32[]{:T(128)}, f32[16,64,4,1024]{3,2,1,0:T(4,128)}, s32[16,64,1024]{2,1,0:T(8,128)}, f32[32,4]{0,1:T(4,128)S(1)}, s32[]{:T(128)}) while((s32[]{:T(128)}, f32[16,64,4,1024]{3,2,1,0:T(4,128)}, s32[16,64,1024]{2,1,0:T(8,128)}, f32[32,4]{0,1:T(4,128)S(1)}, s32[]{:T(128)}) %tuple.173), condition=%wide.region_1.2_spmd.clone, body=%wide.region_0.1_spmd.clone.sunk | while | flops 102760448 | bytes 1835597 | solution.py:88
  137.1 41.2 %all-gather.23.cloned.1.call-done = bf16[2048,640]{1,0:T(8,128)(2,1)} async-done(((bf16[512,640]{1,0:T(8,128)(2,1)}), bf16[2048,640]{1,0:T(8,128)(2,1)}) %all-gather.23.cloned.1.call-update) | async-done | bytes 2621456 | tf_op jit(solution)/shard_map/all_gather | solution.py:137
  206.4 41.2 %all-gather.19.cloned.1.call-done = bf16[640,2048]{1,0:T(8,128)(2,1)} async-done(((bf16[640,512]{1,0:T(8,128)(2,1)}), bf16[640,2048]{1,0:T(8,128)(2,1)}) %all-gather.19.cloned.1.call-update) | async-done | bytes 2621456 | tf_op jit(solution)/shard_map/all_gather | solution.py:138
  255.5 2420.8 %while.54 = (s32[]{:T(128)}, f32[2048,768]{1,0:T(8,128)}, f32[256,2048]{1,0:T(8,128)}, f32[2048,1280]{1,0:T(8,128)}, f32[640,2048]{1,0:T(8,128)}, /*index=5*/f32...) while((s32[]{:T(128)}, f32[2048,768]{1,0:T(8,128)}, ...), condition=%wide.region_19.20_spmd.clone, body=%wide.region_2.19_spmd.clone.sunk | while | flops 40511991808 | bytes 889028736 | solution.py:273
  258.9 47.0 %all-gather.25.cloned.1.call-done = bf16[1024,2048]{1,0:T(8,128)(2,1)} async-done(((bf16[128,2048]{1,0:T(8,128)(2,1)}), bf16[1024,2048]{1,0:T(8,128)(2,1)}) %all-gather.25.cloned.1.call-update) | async-done | bytes 4194320 | tf_op jit(solution)/shard_map/while/body/eval_jaxpr/all_gather | solution.py:57
  337.6 88.5 %reduce-scatter.27.cloned.1.call-done = f32[128,2048]{1,0:T(8,128)} async-done(((f32[1024,2048]{1,0:T(8,128)}), f32[128,2048]{1,0:T(8,128)}) %reduce-scatter.27.cloned.1.call-update) | async-done | bytes 1048592 | tf_op jit(solution)/shard_map/while/body/eval_jaxpr/reduce_scatter | solution.py:65
  434.4 59.2 %collective-permute-done.1 = bf16[256,2048]{1,0:T(8,128)(2,1)} collective-permute-done((bf16[256,2048]{1,0:T(8,128)(2,1)}, bf16[256,2048]{1,0:T(8,128)(2,1)}, u32[]{:S(2)}, u32[]{:S(2)}) %collective-permute-start.1) | collective-permute-done | bytes 1048608 | tf_op jit(solution)/shard_map/while/body/eval_jaxpr/ppermute | solution.py:17
  507.4 83.2 %collective-permute-done.2 = bf16[512,2048]{1,0:T(8,128)(2,1)} collective-permute-done((bf16[512,2048]{1,0:T(8,128)(2,1)}, bf16[512,2048]{1,0:T(8,128)(2,1)}, u32[]{:S(2)}, u32[]{:S(2)}) %collective-permute-start.2) | collective-permute-done | bytes 2097184 | tf_op jit(solution)/shard_map/while/body/eval_jaxpr/ppermute | solution.py:17
  609.7 88.5 %reduce-scatter.29.cloned.1.call-done = f32[128,2048]{1,0:T(8,128)} async-done(((f32[1024,2048]{1,0:T(8,128)}), f32[128,2048]{1,0:T(8,128)}) %reduce-scatter.29.cloned.1.call-update) | async-done | bytes 1048592 | tf_op jit(solution)/shard_map/while/body/eval_jaxpr/reduce_scatter | solution.py:74
  704.4 25.2 collective-permute-done.4
  731.3 92.0 %collective-permute-done.5 = bf16[512,2048]{1,0:T(8,128)(2,1)S(1)} collective-permute-done((bf16[512,2048]{1,0:T(8,128)(2,1)S(1)}, bf16[512,2048]{1,0:T(8,128)(2,1)S(1)}, u32[]{:S(2)}, u32[]{:S(2)}) %collective-permute-start.5) | collective-permute-done | bytes 2097184 | tf_op jit(solution)/shard_map/while/body/eval_jaxpr/ppermute | solution.py:17
  915.6 52.0 %reduce-scatter.31.cloned.1.call-done = f32[128,2048]{1,0:T(8,128)} async-done(((f32[1024,2048]{1,0:T(8,128)}), f32[128,2048]{1,0:T(8,128)}) %reduce-scatter.31.cloned.1.call-update) | async-done | bytes 1048592 | tf_op jit(solution)/shard_map/while/body/eval_jaxpr/reduce_scatter | solution.py:74
  969.4 88.5 %reduce-scatter.33.cloned.1.call-done = f32[128,2048]{1,0:T(8,128)} async-done(((f32[1024,2048]{1,0:T(8,128)}), f32[128,2048]{1,0:T(8,128)}) %reduce-scatter.33.cloned.1.call-update) | async-done | bytes 1048592 | tf_op jit(solution)/shard_map/while/body/eval_jaxpr/reduce_scatter | solution.py:65
  1064.9 45.4 %all-gather.25.cloned.1.call-done = bf16[1024,2048]{1,0:T(8,128)(2,1)} async-done(((bf16[128,2048]{1,0:T(8,128)(2,1)}), bf16[1024,2048]{1,0:T(8,128)(2,1)}) %all-gather.25.cloned.1.call-update) | async-done | bytes 4194320 | tf_op jit(solution)/shard_map/while/body/eval_jaxpr/all_gather | solution.py:57
  1142.1 88.4 %reduce-scatter.27.cloned.1.call-done = f32[128,2048]{1,0:T(8,128)} async-done(((f32[1024,2048]{1,0:T(8,128)}), f32[128,2048]{1,0:T(8,128)}) %reduce-scatter.27.cloned.1.call-update) | async-done | bytes 1048592 | tf_op jit(solution)/shard_map/while/body/eval_jaxpr/reduce_scatter | solution.py:65
  1238.8 59.2 %collective-permute-done.1 = bf16[256,2048]{1,0:T(8,128)(2,1)} collective-permute-done((bf16[256,2048]{1,0:T(8,128)(2,1)}, bf16[256,2048]{1,0:T(8,128)(2,1)}, u32[]{:S(2)}, u32[]{:S(2)}) %collective-permute-start.1) | collective-permute-done | bytes 1048608 | tf_op jit(solution)/shard_map/while/body/eval_jaxpr/ppermute | solution.py:17
  1311.9 83.2 %collective-permute-done.2 = bf16[512,2048]{1,0:T(8,128)(2,1)} collective-permute-done((bf16[512,2048]{1,0:T(8,128)(2,1)}, bf16[512,2048]{1,0:T(8,128)(2,1)}, u32[]{:S(2)}, u32[]{:S(2)}) %collective-permute-start.2) | collective-permute-done | bytes 2097184 | tf_op jit(solution)/shard_map/while/body/eval_jaxpr/ppermute | solution.py:17
  1414.1 88.5 %reduce-scatter.29.cloned.1.call-done = f32[128,2048]{1,0:T(8,128)} async-done(((f32[1024,2048]{1,0:T(8,128)}), f32[128,2048]{1,0:T(8,128)}) %reduce-scatter.29.cloned.1.call-update) | async-done | bytes 1048592 | tf_op jit(solution)/shard_map/while/body/eval_jaxpr/reduce_scatter | solution.py:74
  1535.8 92.0 %collective-permute-done.5 = bf16[512,2048]{1,0:T(8,128)(2,1)S(1)} collective-permute-done((bf16[512,2048]{1,0:T(8,128)(2,1)S(1)}, bf16[512,2048]{1,0:T(8,128)(2,1)S(1)}, u32[]{:S(2)}, u32[]{:S(2)}) %collective-permute-start.5) | collective-permute-done | bytes 2097184 | tf_op jit(solution)/shard_map/while/body/eval_jaxpr/ppermute | solution.py:17
  1726.3 45.7 %reduce-scatter.31.cloned.1.call-done = f32[128,2048]{1,0:T(8,128)} async-done(((f32[1024,2048]{1,0:T(8,128)}), f32[128,2048]{1,0:T(8,128)}) %reduce-scatter.31.cloned.1.call-update) | async-done | bytes 1048592 | tf_op jit(solution)/shard_map/while/body/eval_jaxpr/reduce_scatter | solution.py:74
  1773.8 88.5 %reduce-scatter.33.cloned.1.call-done = f32[128,2048]{1,0:T(8,128)} async-done(((f32[1024,2048]{1,0:T(8,128)}), f32[128,2048]{1,0:T(8,128)}) %reduce-scatter.33.cloned.1.call-update) | async-done | bytes 1048592 | tf_op jit(solution)/shard_map/while/body/eval_jaxpr/reduce_scatter | solution.py:65
  1869.4 45.4 %all-gather.25.cloned.1.call-done = bf16[1024,2048]{1,0:T(8,128)(2,1)} async-done(((bf16[128,2048]{1,0:T(8,128)(2,1)}), bf16[1024,2048]{1,0:T(8,128)(2,1)}) %all-gather.25.cloned.1.call-update) | async-done | bytes 4194320 | tf_op jit(solution)/shard_map/while/body/eval_jaxpr/all_gather | solution.py:57
  1946.5 88.4 %reduce-scatter.27.cloned.1.call-done = f32[128,2048]{1,0:T(8,128)} async-done(((f32[1024,2048]{1,0:T(8,128)}), f32[128,2048]{1,0:T(8,128)}) %reduce-scatter.27.cloned.1.call-update) | async-done | bytes 1048592 | tf_op jit(solution)/shard_map/while/body/eval_jaxpr/reduce_scatter | solution.py:65
  2043.3 59.2 %collective-permute-done.1 = bf16[256,2048]{1,0:T(8,128)(2,1)} collective-permute-done((bf16[256,2048]{1,0:T(8,128)(2,1)}, bf16[256,2048]{1,0:T(8,128)(2,1)}, u32[]{:S(2)}, u32[]{:S(2)}) %collective-permute-start.1) | collective-permute-done | bytes 1048608 | tf_op jit(solution)/shard_map/while/body/eval_jaxpr/ppermute | solution.py:17
  2116.3 83.2 %collective-permute-done.2 = bf16[512,2048]{1,0:T(8,128)(2,1)} collective-permute-done((bf16[512,2048]{1,0:T(8,128)(2,1)}, bf16[512,2048]{1,0:T(8,128)(2,1)}, u32[]{:S(2)}, u32[]{:S(2)}) %collective-permute-start.2) | collective-permute-done | bytes 2097184 | tf_op jit(solution)/shard_map/while/body/eval_jaxpr/ppermute | solution.py:17
  2218.6 88.5 %reduce-scatter.29.cloned.1.call-done = f32[128,2048]{1,0:T(8,128)} async-done(((f32[1024,2048]{1,0:T(8,128)}), f32[128,2048]{1,0:T(8,128)}) %reduce-scatter.29.cloned.1.call-update) | async-done | bytes 1048592 | tf_op jit(solution)/shard_map/while/body/eval_jaxpr/reduce_scatter | solution.py:74
  2340.3 92.0 %collective-permute-done.5 = bf16[512,2048]{1,0:T(8,128)(2,1)S(1)} collective-permute-done((bf16[512,2048]{1,0:T(8,128)(2,1)S(1)}, bf16[512,2048]{1,0:T(8,128)(2,1)S(1)}, u32[]{:S(2)}, u32[]{:S(2)}) %collective-permute-start.5) | collective-permute-done | bytes 2097184 | tf_op jit(solution)/shard_map/while/body/eval_jaxpr/ppermute | solution.py:17
  2530.8 45.7 %reduce-scatter.31.cloned.1.call-done = f32[128,2048]{1,0:T(8,128)} async-done(((f32[1024,2048]{1,0:T(8,128)}), f32[128,2048]{1,0:T(8,128)}) %reduce-scatter.31.cloned.1.call-update) | async-done | bytes 1048592 | tf_op jit(solution)/shard_map/while/body/eval_jaxpr/reduce_scatter | solution.py:74
  2578.3 88.5 %reduce-scatter.33.cloned.1.call-done = f32[128,2048]{1,0:T(8,128)} async-done(((f32[1024,2048]{1,0:T(8,128)}), f32[128,2048]{1,0:T(8,128)}) %reduce-scatter.33.cloned.1.call-update) | async-done | bytes 1048592 | tf_op jit(solution)/shard_map/while/body/eval_jaxpr/reduce_scatter | solution.py:65
  2719.1 104.5 %while.55 = (s32[]{:T(128)}, f32[32,4]{0,1:T(4,128)S(1)}, s32[16,64,1024]{2,1,0:T(8,128)}, f32[16,64,4,1024]{3,2,1,0:T(4,128)}, s32[]{:T(128)}, /*index=5*/s32[]{:T(128)}) while((s32[]{:T(128)}, f32[32,4]{0,1:T(4,128)S(1)}, s32[16,64,1024]{2,1,0:T(8,128)}, f32[16,64,4,1024]{3,2,1,0:T(4,128)}, s32[]{:T(128)}, ...), condition=%wide.region_30.31_spmd.clone, body=%wide.region_29.30_spmd.clone.sunk | while | flops 102760704 | bytes 1836127 | solution.py:110
  2833.3 38.3 %all-reduce.1 = (f32[2048]{0:T(1024)}, f32[2048]{0:T(1024)}) all-reduce(f32[2048]{0:T(1024)S(1)} %copy-done.27, f32[2048]{0:T(1024)S(1)} %copy-done.24), channel_id=1, replica_groups=mesh['dp'=4,'tensor'=8] {'dp','tensor'}, use_global_device_ids=true, to_apply=%region_20.21 | all-reduce | flops 4096 | bytes 32768 | tf_op jit(solution)/shard_map/psum | solution.py:308
  2888.8 40.4 %reduce-scatter.23.cloned.1.call-done = bf16[512,640]{1,0:T(8,128)(2,1)} async-done(((bf16[2048,640]{1,0:T(8,128)(2,1)}), bf16[512,640]{1,0:T(8,128)(2,1)}) %reduce-scatter.23.cloned.1.call-update) | async-done | bytes 655376 | tf_op jit(solution)/shard_map/reduce_scatter | solution.py:298
  (668 shorter events, 947.2 us)
Async XLA Ops:
  7.2 107.2 %all-gather.11.cloned.1.call-start = ((), (), s32[]{:S(2)}) async-start(), calls=%async_computation.11 | async-start | bytes 1310720 | tf_op jit(solution)/shard_map/all_gather | solution.py:132
  7.9 106.5 %all-gather.13.cloned.1.call-start = ((), (), s32[]{:S(2)}) async-start(), calls=%async_computation.12 | async-start | bytes 1310720 | tf_op jit(solution)/shard_map/all_gather | solution.py:133
  8.7 105.7 %all-gather.15.cloned.1.call-start = ((), (), s32[]{:S(2)}) async-start(), calls=%async_computation.13 | async-start | bytes 1310720 | tf_op jit(solution)/shard_map/all_gather | solution.py:134
  9.4 127.7 %all-gather.21.cloned.1.call-start = ((), (), s32[]{:S(2)}) async-start(), calls=%async_computation.16 | async-start | bytes 3276800 | tf_op jit(solution)/shard_map/all_gather | solution.py:136
  10.0 168.3 %all-gather.23.cloned.1.call-start = ((), (), s32[]{:S(2)}) async-start(), calls=%async_computation.17 | async-start | bytes 3276800 | tf_op jit(solution)/shard_map/all_gather | solution.py:137
  10.6 195.8 %all-gather.17.cloned.1.call-start = ((), (), s32[]{:S(2)}) async-start(), calls=%async_computation.14 | async-start | bytes 1310720 | tf_op jit(solution)/shard_map/all_gather | solution.py:135
  11.1 236.5 %all-gather.19.cloned.1.call-start = ((), (), s32[]{:S(2)}) async-start(), calls=%async_computation.15 | async-start | bytes 3276800 | tf_op jit(solution)/shard_map/all_gather | solution.py:138
  258.8 167.2 %reduce-scatter.27.cloned.1.call-start = ((), (), s32[]{:S(2)}) async-start(), calls=%async_computation.26 | async-start | bytes 9437184 | tf_op jit(solution)/shard_map/while/body/eval_jaxpr/reduce_scatter | solution.py:65
  337.5 160.7 %all-gather.27.cloned.1.call-start = ((), (), s32[]{:S(2)}) async-start(), calls=%async_computation.27 | async-start | bytes 4718592 | tf_op jit(solution)/shard_map/while/body/eval_jaxpr/all_gather | solution.py:57
  428.6 269.6 %reduce-scatter.29.cloned.1.call-start = ((), (), s32[]{:S(2)}) async-start(), calls=%async_computation.28 | async-start | bytes 9437184 | tf_op jit(solution)/shard_map/while/body/eval_jaxpr/reduce_scatter | solution.py:74
  609.5 358.1 %reduce-scatter.31.cloned.1.call-start = ((), (), s32[]{:S(2)}) async-start(), calls=%async_computation.29 | async-start | bytes 9437184 | tf_op jit(solution)/shard_map/while/body/eval_jaxpr/reduce_scatter | solution.py:74
  730.6 92.7 %collective-permute-start.5 = (bf16[512,2048]{1,0:T(8,128)(2,1)S(1)}, bf16[512,2048]{1,0:T(8,128)(2,1)S(1)}, u32[]{:S(2)}, u32[]{:S(2)}) collective-permute-start(bf16[512,2048]{1,0:T(8,128)(2,1)S(1)} %maximum_select_fusion.23), channel_id=1, source_target_pairs={{0,4},{1,5},{2,6},{3,7},{4,0},{5,1},{6,2},{7,3},{8,12},{9,13},{10,... | collective-permute-start | bytes 6291464 | tf_op jit(solution)/shard_map/while/body/eval_jaxpr/ppermute | solution.py:17
  879.4 178.5 %reduce-scatter.33.cloned.1.call-start = ((), (), s32[]{:S(2)}) async-start(), calls=%async_computation.30 | async-start | bytes 9437184 | tf_op jit(solution)/shard_map/while/body/eval_jaxpr/reduce_scatter | solution.py:65
  1064.8 165.6 %reduce-scatter.27.cloned.1.call-start = ((), (), s32[]{:S(2)}) async-start(), calls=%async_computation.26 | async-start | bytes 9437184 | tf_op jit(solution)/shard_map/while/body/eval_jaxpr/reduce_scatter | solution.py:65
  1142.0 160.7 %all-gather.27.cloned.1.call-start = ((), (), s32[]{:S(2)}) async-start(), calls=%async_computation.27 | async-start | bytes 4718592 | tf_op jit(solution)/shard_map/while/body/eval_jaxpr/all_gather | solution.py:57
  1233.0 269.6 %reduce-scatter.29.cloned.1.call-start = ((), (), s32[]{:S(2)}) async-start(), calls=%async_computation.28 | async-start | bytes 9437184 | tf_op jit(solution)/shard_map/while/body/eval_jaxpr/reduce_scatter | solution.py:74
  1413.9 358.1 %reduce-scatter.31.cloned.1.call-start = ((), (), s32[]{:S(2)}) async-start(), calls=%async_computation.29 | async-start | bytes 9437184 | tf_op jit(solution)/shard_map/while/body/eval_jaxpr/reduce_scatter | solution.py:74
  1535.1 92.7 %collective-permute-start.5 = (bf16[512,2048]{1,0:T(8,128)(2,1)S(1)}, bf16[512,2048]{1,0:T(8,128)(2,1)S(1)}, u32[]{:S(2)}, u32[]{:S(2)}) collective-permute-start(bf16[512,2048]{1,0:T(8,128)(2,1)S(1)} %maximum_select_fusion.23), channel_id=1, source_target_pairs={{0,4},{1,5},{2,6},{3,7},{4,0},{5,1},{6,2},{7,3},{8,12},{9,13},{10,... | collective-permute-start | bytes 6291464 | tf_op jit(solution)/shard_map/while/body/eval_jaxpr/ppermute | solution.py:17
  1683.9 178.5 %reduce-scatter.33.cloned.1.call-start = ((), (), s32[]{:S(2)}) async-start(), calls=%async_computation.30 | async-start | bytes 9437184 | tf_op jit(solution)/shard_map/while/body/eval_jaxpr/reduce_scatter | solution.py:65
  1869.3 165.6 %reduce-scatter.27.cloned.1.call-start = ((), (), s32[]{:S(2)}) async-start(), calls=%async_computation.26 | async-start | bytes 9437184 | tf_op jit(solution)/shard_map/while/body/eval_jaxpr/reduce_scatter | solution.py:65
  1946.5 160.7 %all-gather.27.cloned.1.call-start = ((), (), s32[]{:S(2)}) async-start(), calls=%async_computation.27 | async-start | bytes 4718592 | tf_op jit(solution)/shard_map/while/body/eval_jaxpr/all_gather | solution.py:57
  2037.5 269.6 %reduce-scatter.29.cloned.1.call-start = ((), (), s32[]{:S(2)}) async-start(), calls=%async_computation.28 | async-start | bytes 9437184 | tf_op jit(solution)/shard_map/while/body/eval_jaxpr/reduce_scatter | solution.py:74
  2218.4 358.1 %reduce-scatter.31.cloned.1.call-start = ((), (), s32[]{:S(2)}) async-start(), calls=%async_computation.29 | async-start | bytes 9437184 | tf_op jit(solution)/shard_map/while/body/eval_jaxpr/reduce_scatter | solution.py:74
  2339.6 92.7 %collective-permute-start.5 = (bf16[512,2048]{1,0:T(8,128)(2,1)S(1)}, bf16[512,2048]{1,0:T(8,128)(2,1)S(1)}, u32[]{:S(2)}, u32[]{:S(2)}) collective-permute-start(bf16[512,2048]{1,0:T(8,128)(2,1)S(1)} %maximum_select_fusion.23), channel_id=1, source_target_pairs={{0,4},{1,5},{2,6},{3,7},{4,0},{5,1},{6,2},{7,3},{8,12},{9,13},{10,... | collective-permute-start | bytes 6291464 | tf_op jit(solution)/shard_map/while/body/eval_jaxpr/ppermute | solution.py:17
  2488.4 178.5 %reduce-scatter.33.cloned.1.call-start = ((), (), s32[]{:S(2)}) async-start(), calls=%async_computation.30 | async-start | bytes 9437184 | tf_op jit(solution)/shard_map/while/body/eval_jaxpr/reduce_scatter | solution.py:65
  2676.3 195.9 %reduce-scatter.19.cloned.1.call-start = ((), (), s32[]{:S(2)}) async-start(), calls=%async_computation.21 | async-start | bytes 1310720 | tf_op jit(solution)/shard_map/reduce_scatter | solution.py:292
  2679.2 194.9 %reduce-scatter.13.cloned.1.call-start = ((), (), s32[]{:S(2)}) async-start(), calls=%async_computation.18 | async-start | bytes 1310720 | tf_op jit(solution)/shard_map/reduce_scatter | solution.py:277
  2684.1 191.8 %reduce-scatter.15.cloned.1.call-start = ((), (), s32[]{:S(2)}) async-start(), calls=%async_computation.19 | async-start | bytes 1310720 | tf_op jit(solution)/shard_map/reduce_scatter | solution.py:280
  2684.8 192.9 %reduce-scatter.17.cloned.1.call-start = ((), (), s32[]{:S(2)}) async-start(), calls=%async_computation.20 | async-start | bytes 1310720 | tf_op jit(solution)/shard_map/reduce_scatter | solution.py:286
  2685.5 193.9 %reduce-scatter.25.cloned.1.call-start = ((), (), s32[]{:S(2)}) async-start(), calls=%async_computation.24 | async-start | bytes 3276800 | tf_op jit(solution)/shard_map/reduce_scatter | solution.py:301
  2690.0 196.5 %reduce-scatter.21.cloned.1.call-start = ((), (), s32[]{:S(2)}) async-start(), calls=%async_computation.22 | async-start | bytes 3276800 | tf_op jit(solution)/shard_map/reduce_scatter | solution.py:295
  2697.5 231.7 %reduce-scatter.23.cloned.1.call-start = ((), (), s32[]{:S(2)}) async-start(), calls=%async_computation.23 | async-start | bytes 3276800 | tf_op jit(solution)/shard_map/reduce_scatter | solution.py:298
  (164 other events, 6689.9 us)
Sparse Core Ops, SparseCore 0:
  9.8 29.2 all-gather.10
  40.9 26.4 all-gather.12
  69.3 26.4 all-gather.14
  97.5 39.4 all-gather.20
  138.8 39.4 all-gather.22
  180.0 26.3 all-gather.16
  208.2 39.3 all-gather.18
  258.9 46.8 all-gather.24
  337.6 88.3 reduce-scatter.26
  428.7 62.7 all-gather.26
  609.6 88.5 reduce-scatter.28
  879.5 88.0 reduce-scatter.30
  969.9 87.9 reduce-scatter.32
  1065.0 45.3 all-gather.24
  1142.1 88.3 reduce-scatter.26
  1233.2 62.7 all-gather.26
  1414.0 88.5 reduce-scatter.28
  1684.0 87.9 reduce-scatter.30
  1774.3 87.9 reduce-scatter.32
  1869.4 45.3 all-gather.24
  1946.6 88.3 reduce-scatter.26
  2037.6 62.7 all-gather.26
  2218.5 88.5 reduce-scatter.28
  2488.5 87.9 reduce-scatter.30
  2578.8 87.9 reduce-scatter.32
  2679.7 26.3 reduce-scatter.18
  2709.5 27.9 reduce-scatter.12
  2740.9 27.9 reduce-scatter.14
  2772.3 27.9 reduce-scatter.16
  2803.2 40.1 reduce-scatter.24
  2846.3 40.1 reduce-scatter.20
  2889.5 39.5 reduce-scatter.22
